TPU v7x, 256 devices: a whole 4x4x8 slice. The times are simulated.
256 devices in a mesh: mp: 2 (over x_hi), row: 8 (over z), col: 16 (over x_lo, y, core).
Axes of the slice: x: 4 (x_hi: 2, x_lo: 2; x = x_hi * 2 + x_lo), y: 4, z: 8, core: 2. Of those that a mesh axis runs over, the one named last changes fastest.
Arguments:
- gram_tiles: bfloat16 [4, 16, 8, 128, 16384], P('mp', None, 'row', None, 'col'), may hold values from -4 to 64, as said below
- weights: bfloat16 [4, 16384, 128], P('mp', ('col', 'row')), may hold values from -8 to 8
- damping: float32 [128], replicated, may hold values from 0.5 to 4
Outputs:
- merged: float32 [16384, 128], P(('col', 'row'))
- residual: float32 [16384, 128], P(('col', 'row'))
Inputs may be any that keep to these rules, and one draw needn't show every extreme that they name: `gram_tiles`: each model's 16384 x 16384 Gram, read as in the first step, is symmetric positive definite.
All inputs are finite; a program needn't handle non-finite values.
Results may differ from a plain program's by a relative error of at most 0.012.
The roundings to bfloat16 on the way count: a program that leaves them out, or rounds other values in their place, can miss the bound.
Values may be sent and summed in bfloat16 or wider, within the bound.
No kernel may reach another device: no remote copies, remote signals or barrier semaphores. Data moves between devices by JAX's collectives and lax.ppermute only.
A program may use at most 64 MiB of HBM per device.

v0:
```python
import jax
import jax.numpy as jnp
from jax import lax
from jax.sharding import PartitionSpec as P

ITERS = 2


def contract_rows(gram_tile, portion):
    spread = jnp.broadcast_to(portion, (gram_tile.shape[0],) + portion.shape[1:])
    return jnp.einsum("mij,mjk->ik", gram_tile, spread, preferred_element_type=jnp.float32)


def apply_models(gram_tile, vectors):
    partial_value = contract_rows(gram_tile, lax.all_gather(vectors, "row", axis=1, tiled=True))
    summed = lax.psum_scatter(partial_value, "col", scatter_dimension=0, tiled=True)
    return (lax.psum(summed, "mp"), partial_value)


def squares(residual):
    return lax.psum(jnp.sum(residual * residual, axis=0), ("row", "col"))


def on_device(gram_tiles, weights, damping):
    shape_in = gram_tiles.shape
    gram_tile = gram_tiles.reshape(
        shape_in[0], shape_in[1] * shape_in[2] * shape_in[3], shape_in[4]
    )
    target, unused = apply_models(gram_tile, weights)
    merged = jnp.zeros_like(target)
    residual = target
    direction = target
    norm_now = squares(residual)
    for iteration in range(ITERS):
        low_dir = direction.astype(jnp.bfloat16)
        applied, partial_value = apply_models(gram_tile, low_dir[None])
        dir_wide = low_dir.astype(jnp.float32)
        applied = applied + damping[None, :] * dir_wide
        curve_term = lax.psum(jnp.sum(dir_wide * applied, axis=0), ("row", "col"))
        step_size = norm_now / curve_term
        merged = merged + step_size[None, :] * direction
        residual = residual - step_size[None, :] * applied
        if iteration + 1 < ITERS:
            norm_next = squares(residual)
            direction = residual + (norm_next / norm_now)[None, :] * direction
            norm_now = norm_next
    return (merged, residual)


def solution(mesh):
    in_specs = (P("mp", None, "row", None, "col"), P("mp", ("col", "row"), None), P())
    out_specs = (P(("col", "row"), None), P(("col", "row"), None))
    return jax.shard_map(
        on_device, mesh=mesh, in_specs=in_specs, out_specs=out_specs, check_vma=False
    )
```

profile of v0, /device:TPU:4, one launch (start us, length us, event | category | flops | bytes accessed | tf_op | source)
XLA Modules:
  0.0 1248.6 jit_solution(5157626509282699537)
XLA Ops:
  7.2 0.0 reduce-scatter.4.cloned.1.call-start
  7.2 29.3 %all_gather.9 = bf16[2,1024,128]{2,1,0:T(8,128)(2,1)S(1)} all-gather(bf16[2,128,128]{2,1,0:T(8,128)(2,1)} %param.4), channel_id=1, replica_groups=mesh['mp'=2,'row'=8,'col'=16] {'row'}, dimensions={1}, use_global_device_ids=true | all-gather | bytes 589824 | tf_op jit(solution)/shard_map/all_gather | solution.py:15
  36.5 6.7 convolution_bitcast_fusion.2
  43.3 0.0 reduce-scatter.4.cloned.1.call-update
  43.3 0.0 copy-start.2
  43.3 0.0 all-reduce.5.cloned.1.call-start
  43.3 63.9 %reduce-scatter.4.cloned.1.call-done = f32[128,128]{1,0:T(8,128)} async-done(((f32[2048,128]{1,0:T(8,128)}), f32[128,128]{1,0:T(8,128)}) %reduce-scatter.4.cloned.1.call-update) | async-done | bytes 65552 | tf_op jit(solution)/shard_map/reduce_scatter | solution.py:16
  107.2 0.0 all-reduce.5.cloned.1.call-update
  107.3 0.0 reduce-scatter.6.cloned.1.call-start
  107.3 33.3 %all-reduce.5.cloned.1.call-done = f32[128,128]{1,0:T(8,128)} async-done(((f32[128,128]{1,0:T(8,128)}), f32[128,128]{1,0:T(8,128)}) %all-reduce.5.cloned.1.call-update) | async-done | bytes 65552 | tf_op jit(solution)/shard_map/psum | solution.py:17
  140.6 0.0 copy-start
  140.6 0.9 convert_element_type.12
  141.5 26.0 %all-gather = bf16[1024,128]{1,0:T(8,128)(2,1)S(1)} all-gather(bf16[128,128]{1,0:T(8,128)(2,1)S(1)} %convert_element_type.12), channel_id=2, replica_groups=mesh['mp'=2,'row'=8,'col'=16] {'row'}, dimensions={0}, use_global_device_ids=true | all-gather | bytes 294912 | tf_op jit(solution)/shard_map/all_gather | solution.py:15
  167.6 0.1 copy.5
  167.7 6.7 convolution_bitcast_fusion.1
  174.4 0.0 reduce-scatter.6.cloned.1.call-update
  174.5 0.0 all-reduce.7.cloned.1.call-start
  174.5 65.0 %reduce-scatter.6.cloned.1.call-done = f32[128,128]{1,0:T(8,128)} async-done(((f32[2048,128]{1,0:T(8,128)}), f32[128,128]{1,0:T(8,128)}) %reduce-scatter.6.cloned.1.call-update) | async-done | bytes 65552 | tf_op jit(solution)/shard_map/reduce_scatter | solution.py:16
  239.6 0.0 all-reduce.7.cloned.1.call-update
  239.6 0.0 reduce-scatter.8.cloned.1.call-start
  239.6 33.3 %all-reduce.7.cloned.1.call-done = f32[128,128]{1,0:T(8,128)} async-done(((f32[128,128]{1,0:T(8,128)}), f32[128,128]{1,0:T(8,128)}) %all-reduce.7.cloned.1.call-update) | async-done | bytes 65552 | tf_op jit(solution)/shard_map/psum | solution.py:17
  272.9 0.0 copy-done.2
  272.9 0.0 copy-done
  272.9 0.9 fusion.3
  273.8 0.0 copy-start.1
  273.8 281.3 %all-reduce = (f32[128]{0:T(128)S(1)}, f32[128]{0:T(128)S(1)}) all-reduce(f32[128]{0:T(128)S(1)} %get-tuple-element.3, f32[128]{0:T(128)S(1)} %get-tuple-element.2), channel_id=1, replica_groups=mesh['mp'=2,'row'=8,'col'=16] {'row','col'}, use_global_device_ids=true, to_apply=%region_3.0 | all-reduce | flops 256 | bytes 2048 | tf_op jit(solution)/shard_map/psum | solution.py:21
  555.1 0.9 multiply_reduce_fusion
  556.0 275.6 %psum.53 = f32[128]{0:T(128)S(1)} all-reduce(f32[128]{0:T(128)S(1)} %multiply_reduce_fusion), channel_id=1, replica_groups=mesh['mp'=2,'row'=8,'col'=16] {'row','col'}, use_global_device_ids=true, to_apply=%region_9.0 | all-reduce | flops 128 | bytes 1024 | tf_op jit(solution)/shard_map/psum | solution.py:21
  831.6 0.9 fusion.6
  832.4 24.9 %all-gather.1 = bf16[1024,128]{1,0:T(8,128)(2,1)S(1)} all-gather(bf16[128,128]{1,0:T(8,128)(2,1)S(1)} %fusion.6), channel_id=3, replica_groups=mesh['mp'=2,'row'=8,'col'=16] {'row'}, dimensions={0}, use_global_device_ids=true | all-gather | bytes 294912 | tf_op jit(solution)/shard_map/all_gather | solution.py:15
  857.3 0.1 copy.7
  857.5 6.7 convolution_bitcast_fusion
  864.2 0.0 reduce-scatter.8.cloned.1.call-update
  864.2 0.0 all-reduce.9.cloned.1.call-start
  864.3 60.5 %reduce-scatter.8.cloned.1.call-done = f32[128,128]{1,0:T(8,128)} async-done(((f32[2048,128]{1,0:T(8,128)}), f32[128,128]{1,0:T(8,128)}) %reduce-scatter.8.cloned.1.call-update) | async-done | bytes 65552 | tf_op jit(solution)/shard_map/reduce_scatter | solution.py:16
  924.8 0.0 all-reduce.9.cloned.1.call-update
  924.8 33.2 %all-reduce.9.cloned.1.call-done = f32[128,128]{1,0:T(8,128)} async-done(((f32[128,128]{1,0:T(8,128)}), f32[128,128]{1,0:T(8,128)}) %all-reduce.9.cloned.1.call-update) | async-done | bytes 65552 | tf_op jit(solution)/shard_map/psum | solution.py:17
  958.1 0.9 fusion.5
  958.9 281.3 %psum.55 = f32[128]{0:T(128)S(1)} all-reduce(f32[128]{0:T(128)S(1)} %fusion.5), channel_id=1, replica_groups=mesh['mp'=2,'row'=8,'col'=16] {'row','col'}, use_global_device_ids=true, to_apply=%region_13.0 | all-reduce | flops 128 | bytes 1024 | tf_op jit(solution)/shard_map/psum | solution.py:39
  1240.2 0.0 copy-done.1
  1240.2 1.5 multiply_subtract_fusion
  (3 shorter events, 0.0 us)
Async XLA Ops:
  7.2 100.1 %reduce-scatter.4.cloned.1.call-start = ((), (), s32[]{:S(2)}) async-start(), calls=%async_computation.3 | async-start | bytes 1114112 | tf_op jit(solution)/shard_map/reduce_scatter | solution.py:16
  43.3 229.6 %copy-start.2 = (f32[128]{0:T(128)S(1)}, f32[128]{0:T(128)}, u32[]{:S(2)}) copy-start(f32[128]{0:T(128)} %param.5) | copy-start | bytes 1540
  43.3 97.3 %all-reduce.5.cloned.1.call-start = ((), (), s32[]{:S(2)}) async-start(), calls=%async_computation.4 | async-start | bytes 131072 | tf_op jit(solution)/shard_map/psum | solution.py:17
  107.3 132.3 %reduce-scatter.6.cloned.1.call-start = ((), (), s32[]{:S(2)}) async-start(), calls=%async_computation.5 | async-start | bytes 1114112 | tf_op jit(solution)/shard_map/reduce_scatter | solution.py:16
  140.6 132.3 %copy-start = (f32[128,128]{1,0:T(8,128)S(1)}, f32[128,128]{1,0:T(8,128)}, u32[]{:S(2)}) copy-start(f32[128,128]{1,0:T(8,128)} %all-reduce.5.cloned.1.call-done) | copy-start | bytes 196612
  174.5 98.5 %all-reduce.7.cloned.1.call-start = ((), (), s32[]{:S(2)}) async-start(), calls=%async_computation.6 | async-start | bytes 131072 | tf_op jit(solution)/shard_map/psum | solution.py:17
  239.6 685.2 %reduce-scatter.8.cloned.1.call-start = ((), (), s32[]{:S(2)}) async-start(), calls=%async_computation.7 | async-start | bytes 1114112 | tf_op jit(solution)/shard_map/reduce_scatter | solution.py:16
  273.8 966.4 %copy-start.1 = (f32[128,128]{1,0:T(8,128)S(1)}, f32[128,128]{1,0:T(8,128)}, u32[]{:S(2)}) copy-start(f32[128,128]{1,0:T(8,128)} %all-reduce.7.cloned.1.call-done) | copy-start | bytes 196612
  864.2 93.9 %all-reduce.9.cloned.1.call-start = ((), (), s32[]{:S(2)}) async-start(), calls=%async_computation.8 | async-start | bytes 131072 | tf_op jit(solution)/shard_map/psum | solution.py:17
Sparse Core Ops, SparseCore 0:
  43.4 63.7 reduce-scatter.3
  109.8 30.8 all-reduce.4
  174.6 64.9 reduce-scatter.5
  242.0 30.9 all-reduce.6
  864.3 60.4 reduce-scatter.7
  927.2 30.8 all-reduce.8
where the time goes:
time: 1250 us
  blocking collectives  918 us (73%)
  waiting for transfers between devices  289 us (23%)
  matrix products  20.2 us (2%)
  between operations  14.1 us (1%)
    psum x2, blocking collectives, squares(): return lax.psum(jnp.sum(residual * residual, axis=0), ('row', 'col'))  557 us
    psum x1, blocking collectives, on_device(): curve_term = lax.psum(jnp.sum(dir_wide * applied, axis=0), ('row', 'col'))  281 us
    reduce_scatter x3, waiting for transfers between devices, apply_models(): lax.psum_scatter(partial_value, 'col', scatter_dimension=0, tiled=True)  189 us
    psum x3, waiting for transfers between devices, apply_models(): return (lax.psum(summed, 'mp'), partial_value)  99.9 us
    all_gather x3, blocking collectives, apply_models(): lax.all_gather(vectors, 'row', axis=1, tiled=True)  80.2 us
  transfers between devices with their start and end apart: 6, of which 6 were waited for; matrix products, arithmetic and copies ran while one was open for 0% of the time, Pallas kernels for 0%

commit v1 on v0

--- a/solution.py
+++ b/solution.py
@@ -36,7 +36,7 @@
         applied, partial_value = apply_models(gram_tile, low_dir[None])
         dir_wide = low_dir.astype(jnp.float32)
         applied = applied + damping[None, :] * dir_wide
-        curve_term = lax.psum(jnp.sum(dir_wide * applied, axis=0), ("row", "col"))
+        curve_term = lax.psum(lax.psum(jnp.sum(dir_wide * applied, axis=0), "col"), axis_name="row")
         step_size = norm_now / curve_term
         merged = merged + step_size[None, :] * direction
         residual = residual - step_size[None, :] * applied

time: 1250 us -> 1060 us (0.85)
  blocking collectives: 918 us -> 726 us
    psum x1 -> x4, blocking collectives: 281 us -> 95.1 us  [the longest x2 60.2 us: on_device(): lax.psum(jnp.sum(dir_wide * applied, axis=0), 'col')]
where the time goes in v1:
time: 1060 us
  blocking collectives  726 us (68%)
  waiting for transfers between devices  290 us (27%)
  matrix products  20.2 us (2%)
  between operations  14.1 us (1%)
    psum x2, blocking collectives, squares(): return lax.psum(jnp.sum(residual * residual, axis=0), ('row', 'col'))  551 us
    reduce_scatter x3, waiting for transfers between devices, apply_models(): lax.psum_scatter(partial_value, 'col', scatter_dimension=0, tiled=True)  190 us
    psum x3, waiting for transfers between devices, apply_models(): return (lax.psum(summed, 'mp'), partial_value)  99.9 us
    all_gather x3, blocking collectives, apply_models(): lax.all_gather(vectors, 'row', axis=1, tiled=True)  80.2 us
    psum x2, blocking collectives, on_device(): lax.psum(jnp.sum(dir_wide * applied, axis=0), 'col')  60.2 us
    psum x2, blocking collectives, on_device(): lax.psum(lax.psum(jnp.sum(dir_wide * applied, axis=0), 'col'), axis_name=...  34.9 us
  transfers between devices with their start and end apart: 6, of which 6 were waited for; matrix products, arithmetic and copies ran while one was open for 0% of the time, Pallas kernels for 0%

profile of v1, /device:TPU:4, one launch (start us, length us, event | category | flops | bytes accessed | tf_op | source)
XLA Modules:
  0.0 1056.9 jit_solution(3575240076810573809)
XLA Ops:
  7.2 0.0 reduce-scatter.4.cloned.1.call-start
  7.2 29.3 %all_gather.9 = bf16[2,1024,128]{2,1,0:T(8,128)(2,1)S(1)} all-gather(bf16[2,128,128]{2,1,0:T(8,128)(2,1)} %param.4), channel_id=1, replica_groups=mesh['mp'=2,'row'=8,'col'=16] {'row'}, dimensions={1}, use_global_device_ids=true | all-gather | bytes 589824 | tf_op jit(solution)/shard_map/all_gather | solution.py:15
  36.5 6.7 convolution_bitcast_fusion.2
  43.3 0.0 reduce-scatter.4.cloned.1.call-update
  43.3 0.0 copy-start.2
  43.3 0.0 all-reduce.4.cloned.1.call-start
  43.3 63.9 %reduce-scatter.4.cloned.1.call-done = f32[128,128]{1,0:T(8,128)} async-done(((f32[2048,128]{1,0:T(8,128)}), f32[128,128]{1,0:T(8,128)}) %reduce-scatter.4.cloned.1.call-update) | async-done | bytes 65552 | tf_op jit(solution)/shard_map/reduce_scatter | solution.py:16
  107.2 0.0 all-reduce.4.cloned.1.call-update
  107.3 0.0 reduce-scatter.6.cloned.1.call-start
  107.3 33.3 %all-reduce.4.cloned.1.call-done = f32[128,128]{1,0:T(8,128)} async-done(((f32[128,128]{1,0:T(8,128)}), f32[128,128]{1,0:T(8,128)}) %all-reduce.4.cloned.1.call-update) | async-done | bytes 65552 | tf_op jit(solution)/shard_map/psum | solution.py:17
  140.6 0.0 copy-start
  140.6 0.9 convert_element_type.12
  141.5 26.0 %all-gather = bf16[1024,128]{1,0:T(8,128)(2,1)S(1)} all-gather(bf16[128,128]{1,0:T(8,128)(2,1)S(1)} %convert_element_type.12), channel_id=2, replica_groups=mesh['mp'=2,'row'=8,'col'=16] {'row'}, dimensions={0}, use_global_device_ids=true | all-gather | bytes 294912 | tf_op jit(solution)/shard_map/all_gather | solution.py:15
  167.6 0.1 copy.5
  167.7 6.7 convolution_bitcast_fusion.1
  174.4 0.0 reduce-scatter.6.cloned.1.call-update
  174.5 0.0 all-reduce.6.cloned.1.call-start
  174.5 65.0 %reduce-scatter.6.cloned.1.call-done = f32[128,128]{1,0:T(8,128)} async-done(((f32[2048,128]{1,0:T(8,128)}), f32[128,128]{1,0:T(8,128)}) %reduce-scatter.6.cloned.1.call-update) | async-done | bytes 65552 | tf_op jit(solution)/shard_map/reduce_scatter | solution.py:16
  239.6 0.0 all-reduce.6.cloned.1.call-update
  239.6 0.0 reduce-scatter.8.cloned.1.call-start
  239.6 33.3 %all-reduce.6.cloned.1.call-done = f32[128,128]{1,0:T(8,128)} async-done(((f32[128,128]{1,0:T(8,128)}), f32[128,128]{1,0:T(8,128)}) %all-reduce.6.cloned.1.call-update) | async-done | bytes 65552 | tf_op jit(solution)/shard_map/psum | solution.py:17
  272.9 0.0 copy-done.2
  272.9 0.0 copy-done
  272.9 0.9 fusion.3
  273.8 0.0 copy-start.1
  273.8 30.1 %psum.66 = f32[128]{0:T(128)S(1)} all-reduce(f32[128]{0:T(128)S(1)} %get-tuple-element.2), channel_id=1, replica_groups=mesh['mp'=2,'row'=8,'col'=16] {'col'}, use_global_device_ids=true, to_apply=%region_7.0 | all-reduce | flops 128 | bytes 1024 | tf_op jit(solution)/shard_map/psum | solution.py:39
  303.9 17.5 %psum.67 = f32[128]{0:T(128)S(1)} all-reduce(f32[128]{0:T(128)S(1)} %psum.66), channel_id=1, replica_groups=mesh['mp'=2,'row'=8,'col'=16] {'row'}, use_global_device_ids=true, to_apply=%region_8.0 | all-reduce | flops 128 | bytes 1024 | tf_op jit(solution)/shard_map/psum | solution.py:39
  321.4 275.6 %psum.64 = f32[128]{0:T(128)S(1)} all-reduce(f32[128]{0:T(128)S(1)} %get-tuple-element.3), channel_id=1, replica_groups=mesh['mp'=2,'row'=8,'col'=16] {'row','col'}, use_global_device_ids=true, to_apply=%region_3.0 | all-reduce | flops 128 | bytes 1024 | tf_op jit(solution)/shard_map/psum | solution.py:21
  597.0 0.9 multiply_reduce_fusion
  597.8 275.6 %psum.68 = f32[128]{0:T(128)S(1)} all-reduce(f32[128]{0:T(128)S(1)} %multiply_reduce_fusion), channel_id=1, replica_groups=mesh['mp'=2,'row'=8,'col'=16] {'row','col'}, use_global_device_ids=true, to_apply=%region_10.0 | all-reduce | flops 128 | bytes 1024 | tf_op jit(solution)/shard_map/psum | solution.py:21
  873.4 0.9 fusion.6
  874.3 24.9 %all-gather.1 = bf16[1024,128]{1,0:T(8,128)(2,1)S(1)} all-gather(bf16[128,128]{1,0:T(8,128)(2,1)S(1)} %fusion.6), channel_id=3, replica_groups=mesh['mp'=2,'row'=8,'col'=16] {'row'}, dimensions={0}, use_global_device_ids=true | all-gather | bytes 294912 | tf_op jit(solution)/shard_map/all_gather | solution.py:15
  899.1 0.1 copy.7
  899.3 6.7 convolution_bitcast_fusion
  906.0 0.0 reduce-scatter.8.cloned.1.call-update
  906.1 0.0 all-reduce.8.cloned.1.call-start
  906.1 60.7 %reduce-scatter.8.cloned.1.call-done = f32[128,128]{1,0:T(8,128)} async-done(((f32[2048,128]{1,0:T(8,128)}), f32[128,128]{1,0:T(8,128)}) %reduce-scatter.8.cloned.1.call-update) | async-done | bytes 65552 | tf_op jit(solution)/shard_map/reduce_scatter | solution.py:16
  966.8 0.0 all-reduce.8.cloned.1.call-update
  966.9 33.2 %all-reduce.8.cloned.1.call-done = f32[128,128]{1,0:T(8,128)} async-done(((f32[128,128]{1,0:T(8,128)}), f32[128,128]{1,0:T(8,128)}) %all-reduce.8.cloned.1.call-update) | async-done | bytes 65552 | tf_op jit(solution)/shard_map/psum | solution.py:17
  1000.1 0.9 fusion.5
  1001.0 30.1 %psum.70 = f32[128]{0:T(128)S(1)} all-reduce(f32[128]{0:T(128)S(1)} %fusion.5), channel_id=1, replica_groups=mesh['mp'=2,'row'=8,'col'=16] {'col'}, use_global_device_ids=true, to_apply=%region_14.0 | all-reduce | flops 128 | bytes 1024 | tf_op jit(solution)/shard_map/psum | solution.py:39
  1031.1 17.5 %psum.71 = f32[128]{0:T(128)S(1)} all-reduce(f32[128]{0:T(128)S(1)} %psum.70), channel_id=1, replica_groups=mesh['mp'=2,'row'=8,'col'=16] {'row'}, use_global_device_ids=true, to_apply=%region_15.0 | all-reduce | flops 128 | bytes 1024 | tf_op jit(solution)/shard_map/psum | solution.py:39
  1048.5 0.0 copy-done.1
  1048.5 1.5 multiply_subtract_fusion
  (3 shorter events, 0.0 us)
Async XLA Ops:
  7.2 100.1 %reduce-scatter.4.cloned.1.call-start = ((), (), s32[]{:S(2)}) async-start(), calls=%async_computation.3 | async-start | bytes 1114112 | tf_op jit(solution)/shard_map/reduce_scatter | solution.py:16
  43.3 229.6 %copy-start.2 = (f32[128]{0:T(128)S(1)}, f32[128]{0:T(128)}, u32[]{:S(2)}) copy-start(f32[128]{0:T(128)} %param.5) | copy-start | bytes 1540
  43.3 97.3 %all-reduce.4.cloned.1.call-start = ((), (), s32[]{:S(2)}) async-start(), calls=%async_computation.4 | async-start | bytes 131072 | tf_op jit(solution)/shard_map/psum | solution.py:17
  107.3 132.3 %reduce-scatter.6.cloned.1.call-start = ((), (), s32[]{:S(2)}) async-start(), calls=%async_computation.5 | async-start | bytes 1114112 | tf_op jit(solution)/shard_map/reduce_scatter | solution.py:16
  140.6 132.3 %copy-start = (f32[128,128]{1,0:T(8,128)S(1)}, f32[128,128]{1,0:T(8,128)}, u32[]{:S(2)}) copy-start(f32[128,128]{1,0:T(8,128)} %all-reduce.4.cloned.1.call-done) | copy-start | bytes 196612
  174.5 98.5 %all-reduce.6.cloned.1.call-start = ((), (), s32[]{:S(2)}) async-start(), calls=%async_computation.6 | async-start | bytes 131072 | tf_op jit(solution)/shard_map/psum | solution.py:17
  239.6 727.2 %reduce-scatter.8.cloned.1.call-start = ((), (), s32[]{:S(2)}) async-start(), calls=%async_computation.7 | async-start | bytes 1114112 | tf_op jit(solution)/shard_map/reduce_scatter | solution.py:16
  273.8 774.7 %copy-start.1 = (f32[128,128]{1,0:T(8,128)S(1)}, f32[128,128]{1,0:T(8,128)}, u32[]{:S(2)}) copy-start(f32[128,128]{1,0:T(8,128)} %all-reduce.6.cloned.1.call-done) | copy-start | bytes 196612
  906.1 94.0 %all-reduce.8.cloned.1.call-start = ((), (), s32[]{:S(2)}) async-start(), calls=%async_computation.8 | async-start | bytes 131072 | tf_op jit(solution)/shard_map/psum | solution.py:17
Sparse Core Ops, SparseCore 0:
  43.4 63.7 reduce-scatter.3
  109.8 30.8 all-reduce.3
  174.6 64.9 reduce-scatter.5
  242.0 30.9 all-reduce.5
  906.2 60.6 reduce-scatter.7
  969.2 30.8 all-reduce.7
